TPU v7x, 32 devices: a whole 2x2x4 slice. The times are simulated.
32 devices in a mesh: orb: 4 (over z), box: 8 (over y, x, core).
Axes of the slice: x: 2, y: 2, z: 4, core: 2. Of those that a mesh axis runs over, the one named last changes fastest.
Arguments:
- coarse: bfloat16 [4, 8, 729, 1024], P('orb', None, None, 'box'), may hold values from -1.5 to 1.5
- wavelets: bfloat16 [4, 7, 729, 1024], P('orb', None, None, 'box'), may hold values from -1.5 to 1.5
- leaf_flags: int32 [4, 1024], P('orb', 'box'), may hold values 0 or 1
- child_key1: int32 [1024], P('box'), may hold values from 0 to 8191, as said below
- child_key2: int32 [2048], P('box'), may hold values from 0 to 8191, as said below
- counts: int32 [8], P('box'), may hold values from 128 to 256, as said below
Outputs:
- density: float32 [729, 2048], P(None, 'box')
Inputs may be any that keep to these rules, and one draw needn't show every extreme that they name: `child_key1`: within each curve range of 128 entries the keys rise and name distinct children; each parent lies in the same range or among the last 32 boxes of the range before; every range but the first has an entry naming a child of the first of those 32 boxes. `child_key2`: within each curve range of 256 entries the keys rise and name distinct children; each parent lies in the same range or among the last 32 boxes of the range before; every range but the first has an entry naming a child of the first of those 32 boxes. `counts`: some range is full in every draw and some range holds the fewest.
All inputs are finite; a program needn't handle non-finite values. No bound on the sum of `leaf_flags` on one device may be relied on, other than what follows from the above.
Results may differ from a plain program's by a relative error of at most 0.0003.
Values may be sent and summed in bfloat16 or wider, within the bound.
A program may use at most 64 MiB of HBM per device.

v0:
```python
import math

import jax
import jax.numpy as jnp
import numpy as np
from jax import lax
from jax.experimental import pallas as pl
from jax.experimental.pallas import tpu as pltpu
from jax.sharding import PartitionSpec as P

SPILL = 32


def legendre_pair(order, where):
    before = where * 0.0 + 1.0
    value = where
    for degree in range(1, order):
        before, value = (value, ((2 * degree + 1) * where * value - degree * before) / (degree + 1))
    return (value, before)


def gauss_rule(order):
    nodes = np.cos(np.pi * (np.arange(order) + 0.75) / (order + 0.5))
    for repeat in range(40):
        value, before = legendre_pair(order, nodes)
        slope = order * (nodes * value - before) / (nodes * nodes - 1.0)
        nodes = nodes - value / slope
    value, before = legendre_pair(order, nodes)
    slope = order * (nodes * value - before) / (nodes * nodes - 1.0)
    weights = 2.0 / ((1.0 - nodes * nodes) * slope * slope)
    return (nodes[::-1], weights[::-1])


def legendre_basis(where):
    shifted = 2.0 * where - 1.0
    rows = [shifted * 0.0 + 1.0, shifted]
    for degree in range(1, 8):
        rows.append(
            ((2 * degree + 1) * shifted * rows[degree] - degree * rows[degree - 1]) / (degree + 1)
        )
    scale = np.sqrt(2.0 * np.arange(9) + 1.0)[:, None]
    return np.stack(rows, 0) * scale


def complement_rows(scaling_rows):
    members = [scaling_rows[index] for index in range(9)]
    kept = []
    identity = np.eye(18)
    for column in range(18):
        vector = identity[column]
        for passes in range(2):
            for member in members + kept:
                vector = vector - np.dot(member, vector) * member
        length = np.sqrt(np.dot(vector, vector))
        if length > 0.1 and len(kept) < 9:
            kept.append(vector / length)
    return np.stack(kept, 0)


def wavelet_tables():
    nodes, weights = gauss_rule(24)
    points = 0.5 * (nodes + 1.0)
    halves = 0.5 * weights
    lower = legendre_basis(0.5 * points) * halves @ legendre_basis(points).T / math.sqrt(2.0)
    upper = legendre_basis(0.5 * points + 0.5) * halves @ legendre_basis(points).T / math.sqrt(2.0)
    scaling_rows = np.concatenate([lower, upper], 1)
    wavelet_rows = complement_rows(scaling_rows)
    matrix = np.concatenate([scaling_rows, wavelet_rows], 0).reshape(2, 9, 2, 9)
    gauss, gauss_weights = gauss_rule(9)
    quad = legendre_basis(0.5 * (gauss + 1.0)).T * np.sqrt(0.5 * gauss_weights)[:, None]
    return (matrix.reshape(18, 2, 9), quad)


ROWS = 729
PADDED = 800
GROUPS = ((0, 1), (2, 3), (4, 5), (6, 7), (8, 9, 10))
QUARTER = 192


def local_keys(keys, boxes):
    key = keys - lax.axis_index("box") * (8 * boxes)
    return (lax.shift_right_arithmetic(key, 3), key & 7)


def spread_matrix(boxes, group):
    source = lax.broadcasted_iota(jnp.int32, (boxes, 128), 0)
    target = lax.broadcasted_iota(jnp.int32, (boxes, 128), 1)
    hit = (source - (boxes - SPILL) == target - SPILL * group) & (source >= boxes - SPILL)
    return hit.astype(jnp.float32).astype(jnp.bfloat16)


def pick_own(column, boxes):
    row = lax.broadcasted_iota(jnp.int32, (boxes, column.shape[1]), 0)
    return (row == column).astype(jnp.float32)


def pick_spilled(column, group):
    row = lax.broadcasted_iota(jnp.int32, (128, column.shape[1]), 0)
    hit = (row == column + SPILL * (group + 1)) & (column < 0)
    return hit.astype(jnp.float32)


def fill_coefficients(coef_ref, octant, table):
    for axis in range(3):
        bit = jnp.broadcast_to((octant >> axis) & 1, (8, 128)) == 1
        for k in range(18):
            for f in range(9):
                coef_ref[axis * 162 + k * 9 + f] = jnp.where(
                    bit, np.float32(table[k, 1, f]), np.float32(table[k, 0, f])
                )


def contract(source_ref, low, high, coef_ref, axis, store):
    for group in GROUPS:
        inputs = [
            [
                source_ref[block, pl.ds(l + 72 * t, 8, stride=9), :]
                for block in (low, high)
                for l in range(9)
            ]
            for t in group
        ]
        for f in range(9):
            sums = [None] * len(group)
            for k in range(18):
                weight = coef_ref[axis * 162 + k * 9 + f]
                for n in range(len(group)):
                    term = weight * inputs[n][k]
                    sums[n] = term if sums[n] is None else sums[n] + term
            for n, t in enumerate(group):
                store(81 * f + 8 * t, min(8, 81 - 8 * t), sums[n])


def lower_axis(source_ref, target_ref, coef_ref, axis, start, stop):
    def step(index, carry):
        def store(row, count, value):
            target_ref[index, row : row + count, :] = value[:count]

        contract(source_ref, 2 * index, 2 * index + 1, coef_ref, axis, store)
        return carry

    lax.fori_loop(start, stop, step, 0)


def dot(left, right):
    return jnp.dot(left, right, preferred_element_type=jnp.float32)


def encode(value):
    top = jnp.max(jnp.abs(value), axis=0, keepdims=True)
    scaled = value * (32767.0 / jnp.maximum(top, 1e-30))
    return (jnp.round(scaled).astype(jnp.int32).astype(jnp.int16), top)


def decode_square(code, top):
    value = code.astype(jnp.int32).astype(jnp.float32) * (top * np.float32(1.0 / 32767.0))
    return value * value


def density_kernel(
    counts_ref, coarse_hbm, waves_hbm, flags_ref, key1_ref, key2_ref, out_ref,
    coarse_ref, waves_ref, pack_ref, halo_ref, fine_ref, spill_ref, spilled_ref,
    x_ref, a_ref, b_ref, coef_ref, value_ref, code_ref, top_ref,
    got_code, got_top, mine_code, mine_top, sum_code, sum_top,
    load_sem, halo_send, halo_recv, code_send, code_recv, top_send, top_recv,
    sum_send, sum_recv, peak_send, peak_recv, *, count, ranges, table, valued
):
    boxes = coarse_ref.shape[-1]
    tiles, padded = code_ref.shape[:2]
    chunk = padded // count
    me, position = lax.axis_index("orb"), lax.axis_index("box")
    after, before = lax.rem(position + 1, ranges), lax.rem(position + ranges - 1, ranges)
    mesh_id = pl.DeviceIdType.MESH
    load_coarse = pltpu.make_async_copy(coarse_hbm, coarse_ref, load_sem.at[0])
    load_waves = pltpu.make_async_copy(waves_hbm, waves_ref, load_sem.at[1])
    load_coarse.start()
    load_waves.start()
    barrier = pltpu.get_barrier_semaphore()
    for d in range(1, count):
        pl.semaphore_signal(barrier, inc=1, device_id={"orb": lax.rem(me + d, count)}, device_id_type=mesh_id)
    for other in (after, before):
        pl.semaphore_signal(barrier, inc=1, device_id={"box": other}, device_id_type=mesh_id)

    def halo(source, target, index):
        return pltpu.make_async_remote_copy(
            src_ref=source,
            dst_ref=target,
            send_sem=halo_send.at[index],
            recv_sem=halo_recv.at[index],
            device_id={"box": after},
            device_id_type=mesh_id,
        )

    def direct(source, target, sends, recvs, d, t):
        return pltpu.make_async_remote_copy(
            src_ref=source,
            dst_ref=target.at[d - 1, t],
            send_sem=sends.at[d - 1, t],
            recv_sem=recvs.at[d - 1, t],
            device_id={"orb": lax.rem(me + d, count)},
            device_id_type=mesh_id,
        )

    def rows(owner):
        return pl.ds(pl.multiple_of(owner * chunk, chunk), chunk)

    def partials(d, t):
        peer = lax.rem(me + d, count)
        return (
            direct(top_ref.at[t], got_top, top_send, top_recv, d, t),
            direct(code_ref.at[t, rows(peer)], got_code, code_send, code_recv, d, t),
        )

    def totals(d, t):
        return (
            direct(mine_top.at[t], sum_top, peak_send, peak_recv, d, t),
            direct(mine_code.at[t], sum_code, sum_send, sum_recv, d, t),
        )

    coarse_halo = halo(pack_ref.at[0], halo_ref.at[0], 0)
    waves_halo = halo(pack_ref.at[1], halo_ref.at[1], 1)
    fine_halo = halo(spill_ref, spilled_ref, 2)
    keep = jnp.broadcast_to((1 - flags_ref[...]).astype(jnp.float32), (16, boxes)).astype(jnp.bfloat16)
    spread = [spread_matrix(boxes, g) for g in range(4)]
    load_coarse.wait()
    for h in range(2):
        total = dot(coarse_ref[0, h], spread[0])
        for g in range(1, 4):
            total = total + dot(coarse_ref[0, 2 * g + h], spread[g])
        pack_ref[0, h] = total.astype(jnp.bfloat16)
    pl.semaphore_wait(barrier, count + 1)
    coarse_halo.start()
    load_waves.wait()
    packed_keep = sum(dot(keep, s) for s in spread)[:1]
    for h in range(2):
        total = None
        for g in range(4):
            if 2 * g + h > 0:
                term = dot(waves_ref[0, 2 * g + h - 1], spread[g])
                total = term if total is None else total + term
        pack_ref[1, h] = (total * packed_keep).astype(jnp.bfloat16)
    column, octant = local_keys(key1_ref[...], boxes)
    fill_coefficients(coef_ref, octant, table)
    own = pick_own(column, boxes)
    waves_halo.start()
    fine_ref[ROWS - 1 : 4 * QUARTER, :] = jnp.zeros((4 * QUARTER - ROWS + 1, 128), jnp.float32)
    value_ref[ROWS - 1 : padded, :] = jnp.zeros((padded - ROWS + 1, 128), jnp.float32)
    coarse_halo.wait_recv()
    for g in range(4):
        pick = jnp.concatenate([own, pick_spilled(column, g)], 0).astype(jnp.bfloat16)
        for h in range(2):
            both = jnp.concatenate([coarse_ref[0, 2 * g + h], halo_ref[0, h]], 1)
            x_ref[2 * g + h, 0:ROWS, :] = dot(both, pick)
    lower_axis(x_ref, a_ref, coef_ref, 0, 0, 4)
    lower_axis(a_ref, b_ref, coef_ref, 1, 0, 2)

    def store_fine(row, rows_in, value):
        fine_ref[row : row + rows_in, :] = value[:rows_in]

    contract(b_ref, 0, 1, coef_ref, 2, store_fine)
    for part in range(2):
        total = None
        for g in range(4):
            quarter = fine_ref[QUARTER * g : QUARTER * (g + 1), :]
            half = quarter.astype(jnp.bfloat16)
            if part == 1:
                half = (quarter - half.astype(jnp.float32)).astype(jnp.bfloat16)
            term = dot(half, spread[g])
            total = term if total is None else total + term
        spill_ref[part] = total.astype(jnp.bfloat16)
    fine_halo.start()

    def leaf_tile(t, carry):
        column, octant = local_keys(key2_ref[t], boxes)
        fill_coefficients(coef_ref, octant, valued)
        own = pick_own(column, boxes)
        own_kept = own * dot(keep, own.astype(jnp.bfloat16))[:1]

        @pl.when(t == 0)
        def arrived_waves():
            waves_halo.wait_recv()

        for g in range(4):
            pick = jnp.concatenate([own_kept, pick_spilled(column, g)], 0).astype(jnp.bfloat16)
            for h in range(2):
                if 2 * g + h > 0:
                    both = jnp.concatenate([waves_ref[0, 2 * g + h - 1], halo_ref[1, h]], 1)
                    x_ref[2 * g + h, 0:ROWS, :] = dot(both, pick)
        lower_axis(x_ref, a_ref, coef_ref, 0, 1, 4)

        @pl.when(t == 0)
        def arrived_fine():
            fine_halo.wait_recv()

        for g in range(4):
            pick = jnp.concatenate([own, pick_spilled(column, g)], 0).astype(jnp.bfloat16)
            quarter = fine_ref[QUARTER * g : QUARTER * (g + 1), :]
            high = quarter.astype(jnp.bfloat16)
            low = (quarter - high.astype(jnp.float32)).astype(jnp.bfloat16)
            total = dot(jnp.concatenate([high, spilled_ref[0]], 1), pick)
            total = total + dot(jnp.concatenate([low, spilled_ref[1]], 1), pick)
            x_ref[0, QUARTER * g : QUARTER * (g + 1), :] = total
        lower_axis(x_ref, a_ref, coef_ref, 0, 0, 1)
        lower_axis(a_ref, b_ref, coef_ref, 1, 0, 2)
        slot = t * 128 + lax.broadcasted_iota(jnp.int32, (8, 128), 1)
        live = jnp.where(slot < counts_ref[0], 1.0, 0.0).astype(jnp.float32)

        def store_value(row, rows_in, value):
            value_ref[row : row + rows_in, :] = (value * live)[:rows_in]

        contract(b_ref, 0, 1, coef_ref, 2, store_value)
        code, top = encode(value_ref[...])
        code_ref[t] = code
        top_ref[t] = jnp.broadcast_to(top, (8, 128))
        for d in range(1, count):
            for copy in partials(d, t):
                copy.start()
        return carry

    lax.fori_loop(0, tiles, leaf_tile, 0)
    for t in range(tiles):
        total = decode_square(code_ref[t, rows(me), :], top_ref[t, 0:1, :])
        for d in range(1, count):
            for copy in partials(d, t):
                copy.wait_recv()
            total = total + decode_square(got_code[d - 1, t], got_top[d - 1, t, 0:1, :])
        code, top = encode(jnp.sqrt(2.0 * total))
        mine_code[t] = code
        mine_top[t] = jnp.broadcast_to(top, (8, 128))
        out_ref[rows(me), 128 * t : 128 * (t + 1)] = decode_square(code, top)
        for d in range(1, count):
            for copy in totals(d, t):
                copy.start()
    for t in range(tiles):
        for d in range(1, count):
            for copy in totals(d, t):
                copy.wait_recv()
            owner = lax.rem(me + count - d, count)
            out_ref[rows(owner), 128 * t : 128 * (t + 1)] = decode_square(
                sum_code[d - 1, t], sum_top[d - 1, t, 0:1, :]
            )
    for copy in (coarse_halo, waves_halo, fine_halo):
        copy.wait_send()
    for t in range(tiles):
        for d in range(1, count):
            for copy in partials(d, t) + totals(d, t):
                copy.wait_send()


def shards(coarse, wavelets, leaf_flags, child_key1, child_key2, counts):
    matrix, quad = wavelet_tables()
    valued = np.einsum("kop,gp->kog", matrix, quad)
    boxes = coarse.shape[-1]
    slots = child_key2.shape[0]
    count, ranges = lax.axis_size("orb"), lax.axis_size("box")
    padded = -(-ROWS // (16 * count)) * 16 * count
    chunk = padded // count
    tiles = slots // 128
    peers = (count - 1, tiles)
    vmem = pl.BlockSpec(memory_space=pltpu.VMEM)
    anywhere = pl.BlockSpec(memory_space=pl.ANY)
    density = pl.pallas_call(
        lambda *refs: density_kernel(*refs, count=count, ranges=ranges, table=matrix, valued=valued),
        out_shape=jax.ShapeDtypeStruct((padded, slots), jnp.float32),
        in_specs=[pl.BlockSpec(memory_space=pltpu.SMEM), anywhere, anywhere, vmem, vmem, vmem],
        out_specs=vmem,
        scratch_shapes=[
            pltpu.VMEM(coarse.shape, jnp.bfloat16),
            pltpu.VMEM(wavelets.shape, jnp.bfloat16),
            pltpu.VMEM((2, 2, ROWS, 128), jnp.bfloat16),
            pltpu.VMEM((2, 2, ROWS, 128), jnp.bfloat16),
            pltpu.VMEM((4 * QUARTER, 128), jnp.float32),
            pltpu.VMEM((2, QUARTER, 128), jnp.bfloat16),
            pltpu.VMEM((2, QUARTER, 128), jnp.bfloat16),
            pltpu.VMEM((8, PADDED, 128), jnp.float32),
            pltpu.VMEM((4, PADDED, 128), jnp.float32),
            pltpu.VMEM((2, PADDED, 128), jnp.float32),
            pltpu.VMEM((3 * 162, 8, 128), jnp.float32),
            pltpu.VMEM((padded, 128), jnp.float32),
            pltpu.VMEM((tiles, padded, 128), jnp.int16),
            pltpu.VMEM((tiles, 8, 128), jnp.float32),
            pltpu.VMEM(peers + (chunk, 128), jnp.int16),
            pltpu.VMEM(peers + (8, 128), jnp.float32),
            pltpu.VMEM((tiles, chunk, 128), jnp.int16),
            pltpu.VMEM((tiles, 8, 128), jnp.float32),
            pltpu.VMEM(peers + (chunk, 128), jnp.int16),
            pltpu.VMEM(peers + (8, 128), jnp.float32),
            pltpu.SemaphoreType.DMA((2,)),
            pltpu.SemaphoreType.DMA((3,)),
            pltpu.SemaphoreType.DMA((3,)),
        ]
        + [pltpu.SemaphoreType.DMA(peers)] * 8,
        compiler_params=pltpu.CompilerParams(
            collective_id=0, has_side_effects=True, vmem_limit_bytes=60 * 1024 * 1024
        ),
    )(
        counts,
        coarse,
        wavelets,
        leaf_flags,
        child_key1.reshape(1, boxes),
        child_key2.reshape(tiles, 1, 128),
    )
    return density[:ROWS]


def solution(mesh):
    in_specs = (
        P("orb", None, None, "box"),
        P("orb", None, None, "box"),
        P("orb", "box"),
        P("box"),
        P("box"),
        P("box"),
    )
    out_specs = P(None, "box")
    return jax.shard_map(shards, mesh=mesh, in_specs=in_specs, out_specs=out_specs, check_vma=False)
```

profile of v0, /device:TPU:0, one launch (start us, length us, event | category | flops | bytes accessed | tf_op | source)
XLA Modules:
  0.0 48.2 jit_solution(7695139578248505211)
XLA Ops:
  0.7 2.7 %copy.7.refs_1_ = bf16[1,8,729,128]{3,2,1,0:T(8,128)(2,1)} copy(bf16[1,8,729,128]{3,1,2,0:T(8,128)(2,1)} %param.6) | data formatting | bytes 2985984 | tf_op args[0]
  3.4 42.8 %shard_map.64 = f32[768,256]{1,0:T(8,128)} custom-call(s32[1]{0:T(128)S(6)} %copy.8.refs_0_, bf16[1,8,729,128]{3,2,1,0:T(8,128)(2,1)} %copy.7.refs_1_, bf16[1,7,729,128]{3,2,1,0:T(8,128)(2,1)} %refs_2_.1, s32[1,128]{1,0:T(1,128)} %refs_3_.1, s32[1,128]{1,0:T(1,128)} %bitcast.3, s32[2,1,128]{2,1,0:T(1,128)} %bitcast.2), custom_call_target="tpu_custom_call" | custom-call | tf_op jit(solution)/shard_map/pallas_call | solution.py:362
  46.2 2.0 %slice.3 = f32[729,256]{1,0:T(8,128)} slice(f32[768,256]{1,0:T(8,128)} %shard_map.64), slice={[0:729], [0:256]} | slice | bytes 1492992 | tf_op jit(solution)/shard_map/slice | solution.py:404
where the time goes:
time: 48.5 us; the launch traced here: 48.2 us
  Pallas kernels  42.8 us (88%)
  local copies, waits for them, and re-layouts  4.77 us (10%)
  between operations  0.66 us (1%)
    pallas_call x1, Pallas kernels, shards(): pl.pallas_call(lambda *refs: density_kernel(*refs, count=count, ranges=ra...  42.8 us
    unnamed x1, local copies, waits for them, and re-layouts  2.73 us
    slice x1, local copies, waits for them, and re-layouts, shards(): return density[:ROWS]  2.04 us

commit v1 on v0

--- a/solution.py
+++ b/solution.py
@@ -73,6 +73,8 @@
 
 ROWS = 729
 PADDED = 800
+SEGMENT = 92
+HALVES = (((0, 1), (2, 3, 4)), ((5, 6), (7, 8), (9, 10)))
 GROUPS = ((0, 1), (2, 3), (4, 5), (6, 7), (8, 9, 10))
 QUARTER = 192
 
@@ -110,16 +112,14 @@
                 )
 
 
-def contract(source_ref, low, high, coef_ref, axis, store):
-    for group in GROUPS:
-        inputs = [
-            [
-                source_ref[block, pl.ds(l + 72 * t, 8, stride=9), :]
-                for block in (low, high)
-                for l in range(9)
-            ]
-            for t in group
-        ]
+def contract(source_ref, low, high, coef_ref, axis, store, groups=GROUPS):
+    def load(block, row):
+        if len(source_ref.shape) == 2:
+            return source_ref[pl.ds(8 * row + block, 8, stride=72), :]
+        return source_ref[block, pl.ds(row, 8, stride=9), :]
+
+    for group in groups:
+        inputs = [[load(block, l + 72 * t) for block in (low, high) for l in range(9)] for t in group]
         for f in range(9):
             sums = [None] * len(group)
             for k in range(18):
@@ -131,12 +131,12 @@
                 store(81 * f + 8 * t, min(8, 81 - 8 * t), sums[n])
 
 
-def lower_axis(source_ref, target_ref, coef_ref, axis, start, stop):
+def lower_axis(source_ref, target_ref, coef_ref, axis, start, stop, groups=GROUPS):
     def step(index, carry):
         def store(row, count, value):
             target_ref[index, row : row + count, :] = value[:count]
 
-        contract(source_ref, 2 * index, 2 * index + 1, coef_ref, axis, store)
+        contract(source_ref, 2 * index, 2 * index + 1, coef_ref, axis, store, groups)
         return carry
 
     lax.fori_loop(start, stop, step, 0)
@@ -158,20 +158,19 @@
 
 
 def density_kernel(
-    counts_ref, coarse_hbm, waves_hbm, flags_ref, key1_ref, key2_ref, out_ref,
-    coarse_ref, waves_ref, pack_ref, halo_ref, fine_ref, spill_ref, spilled_ref,
+    counts_ref, coarse_hbm, waves_hbm, flags_ref, key1_ref, key2_ref, sum_code, sum_top,
+    coarse_ref, waves_ref, coarse_pack_ref, coarse_halo_ref, pack_ref, halo_ref, level_ref, fine_ref, spill_ref, spilled_ref,
     x_ref, a_ref, b_ref, coef_ref, value_ref, code_ref, top_ref,
-    got_code, got_top, mine_code, mine_top, sum_code, sum_top,
-    load_sem, halo_send, halo_recv, code_send, code_recv, top_send, top_recv,
+    got_code, got_top, load_sem, halo_send, halo_recv, code_send, code_recv, top_send, top_recv,
     sum_send, sum_recv, peak_send, peak_recv, *, count, ranges, table, valued
 ):
-    boxes = coarse_ref.shape[-1]
+    boxes = coarse_hbm.shape[-1]
     tiles, padded = code_ref.shape[:2]
     chunk = padded // count
     me, position = lax.axis_index("orb"), lax.axis_index("box")
     after, before = lax.rem(position + 1, ranges), lax.rem(position + ranges - 1, ranges)
     mesh_id = pl.DeviceIdType.MESH
-    load_coarse = pltpu.make_async_copy(coarse_hbm, coarse_ref, load_sem.at[0])
+    load_coarse = pltpu.make_async_copy(coarse_hbm, coarse_ref.at[pl.ds(0, ROWS)], load_sem.at[0])
     load_waves = pltpu.make_async_copy(waves_hbm, waves_ref, load_sem.at[1])
     load_coarse.start()
     load_waves.start()
@@ -194,7 +193,7 @@
     def direct(source, target, sends, recvs, d, t):
         return pltpu.make_async_remote_copy(
             src_ref=source,
-            dst_ref=target.at[d - 1, t],
+            dst_ref=target,
             send_sem=sends.at[d - 1, t],
             recv_sem=recvs.at[d - 1, t],
             device_id={"orb": lax.rem(me + d, count)},
@@ -207,57 +206,72 @@
     def partials(d, t):
         peer = lax.rem(me + d, count)
         return (
-            direct(top_ref.at[t], got_top, top_send, top_recv, d, t),
-            direct(code_ref.at[t, rows(peer)], got_code, code_send, code_recv, d, t),
+            direct(top_ref.at[t], got_top.at[d - 1, t], top_send, top_recv, d, t),
+            direct(code_ref.at[t, rows(peer)], got_code.at[d - 1, t], code_send, code_recv, d, t),
         )
 
     def totals(d, t):
         return (
-            direct(mine_top.at[t], sum_top, peak_send, peak_recv, d, t),
-            direct(mine_code.at[t], sum_code, sum_send, sum_recv, d, t),
+            direct(sum_top.at[me, t], sum_top.at[me, t], peak_send, peak_recv, d, t),
+            direct(sum_code.at[me, t], sum_code.at[me, t], sum_send, sum_recv, d, t),
         )
 
-    coarse_halo = halo(pack_ref.at[0], halo_ref.at[0], 0)
-    waves_halo = halo(pack_ref.at[1], halo_ref.at[1], 1)
-    fine_halo = halo(spill_ref, spilled_ref, 2)
+    coarse_halo = [halo(coarse_pack_ref.at[h], coarse_halo_ref.at[h], h) for h in range(2)]
+    waves_halo = halo(pack_ref, halo_ref, 2)
+    fine_halo = halo(spill_ref, spilled_ref, 3)
     keep = jnp.broadcast_to((1 - flags_ref[...]).astype(jnp.float32), (16, boxes)).astype(jnp.bfloat16)
     spread = [spread_matrix(boxes, g) for g in range(4)]
+    tail = 8 * SEGMENT - ROWS
+    coarse_ref[ROWS : ROWS + tail] = jnp.zeros((tail, 8, boxes), jnp.bfloat16)
+
+    def segment(index):
+        return coarse_ref[SEGMENT * index : SEGMENT * (index + 1)].reshape(8 * SEGMENT, boxes)
+
     load_coarse.wait()
     for h in range(2):
-        total = dot(coarse_ref[0, h], spread[0])
+        total = dot(segment(4 * h), spread[0])
         for g in range(1, 4):
-            total = total + dot(coarse_ref[0, 2 * g + h], spread[g])
-        pack_ref[0, h] = total.astype(jnp.bfloat16)
-    pl.semaphore_wait(barrier, count + 1)
-    coarse_halo.start()
+            total = total + dot(segment(4 * h + g), spread[g])
+        coarse_pack_ref[h] = total.astype(jnp.bfloat16)
+        if h == 0:
+            pl.semaphore_wait(barrier, count + 1)
+        coarse_halo[h].start()
     load_waves.wait()
     packed_keep = sum(dot(keep, s) for s in spread)[:1]
     for h in range(2):
         total = None
         for g in range(4):
-            if 2 * g + h > 0:
-                term = dot(waves_ref[0, 2 * g + h - 1], spread[g])
+            if 4 * h + g > 0:
+                term = dot(waves_ref[0, 4 * h + g - 1], spread[g])
                 total = term if total is None else total + term
-        pack_ref[1, h] = (total * packed_keep).astype(jnp.bfloat16)
+        pack_ref[h] = (total * packed_keep).astype(jnp.bfloat16)
+    waves_halo.start()
     column, octant = local_keys(key1_ref[...], boxes)
-    fill_coefficients(coef_ref, octant, table)
+    fill_coefficients(coef_ref.at[tiles], octant, table)
     own = pick_own(column, boxes)
-    waves_halo.start()
     fine_ref[ROWS - 1 : 4 * QUARTER, :] = jnp.zeros((4 * QUARTER - ROWS + 1, 128), jnp.float32)
     value_ref[ROWS - 1 : padded, :] = jnp.zeros((padded - ROWS + 1, 128), jnp.float32)
-    coarse_halo.wait_recv()
-    for g in range(4):
-        pick = jnp.concatenate([own, pick_spilled(column, g)], 0).astype(jnp.bfloat16)
-        for h in range(2):
-            both = jnp.concatenate([coarse_ref[0, 2 * g + h], halo_ref[0, h]], 1)
-            x_ref[2 * g + h, 0:ROWS, :] = dot(both, pick)
-    lower_axis(x_ref, a_ref, coef_ref, 0, 0, 4)
-    lower_axis(a_ref, b_ref, coef_ref, 1, 0, 2)
+
+    def leaf_coefficients(t, carry):
+        fill_coefficients(coef_ref.at[t], local_keys(key2_ref[t], boxes)[1], valued)
+        return carry
+
+    lax.fori_loop(0, tiles, leaf_coefficients, 0)
+    coef = coef_ref.at[tiles]
+    for h in range(2):
+        coarse_halo[h].wait_recv()
+        for g in range(4):
+            pick = jnp.concatenate([own, pick_spilled(column, g)], 0).astype(jnp.bfloat16)
+            both = jnp.concatenate([segment(4 * h + g), coarse_halo_ref[h]], 1)
+            start = 8 * SEGMENT * (4 * h + g)
+            level_ref[start : start + 8 * SEGMENT, :] = dot(both, pick)
+        lower_axis(level_ref, a_ref, coef, 0, 0, 4, HALVES[h])
+    lower_axis(a_ref, b_ref, coef, 1, 0, 2)
 
     def store_fine(row, rows_in, value):
         fine_ref[row : row + rows_in, :] = value[:rows_in]
 
-    contract(b_ref, 0, 1, coef_ref, 2, store_fine)
+    contract(b_ref, 0, 1, coef, 2, store_fine)
     for part in range(2):
         total = None
         for g in range(4):
@@ -271,8 +285,8 @@
     fine_halo.start()
 
     def leaf_tile(t, carry):
-        column, octant = local_keys(key2_ref[t], boxes)
-        fill_coefficients(coef_ref, octant, valued)
+        column = local_keys(key2_ref[t], boxes)[0]
+        coef = coef_ref.at[t]
         own = pick_own(column, boxes)
         own_kept = own * dot(keep, own.astype(jnp.bfloat16))[:1]
 
@@ -283,10 +297,10 @@
         for g in range(4):
             pick = jnp.concatenate([own_kept, pick_spilled(column, g)], 0).astype(jnp.bfloat16)
             for h in range(2):
-                if 2 * g + h > 0:
-                    both = jnp.concatenate([waves_ref[0, 2 * g + h - 1], halo_ref[1, h]], 1)
-                    x_ref[2 * g + h, 0:ROWS, :] = dot(both, pick)
-        lower_axis(x_ref, a_ref, coef_ref, 0, 1, 4)
+                if 4 * h + g > 0:
+                    both = jnp.concatenate([waves_ref[0, 4 * h + g - 1], halo_ref[h]], 1)
+                    x_ref[4 * h + g, 0:ROWS, :] = dot(both, pick)
+        lower_axis(x_ref, a_ref, coef, 0, 1, 4)
 
         @pl.when(t == 0)
         def arrived_fine():
@@ -300,15 +314,15 @@
             total = dot(jnp.concatenate([high, spilled_ref[0]], 1), pick)
             total = total + dot(jnp.concatenate([low, spilled_ref[1]], 1), pick)
             x_ref[0, QUARTER * g : QUARTER * (g + 1), :] = total
-        lower_axis(x_ref, a_ref, coef_ref, 0, 0, 1)
-        lower_axis(a_ref, b_ref, coef_ref, 1, 0, 2)
+        lower_axis(x_ref, a_ref, coef, 0, 0, 1)
+        lower_axis(a_ref, b_ref, coef, 1, 0, 2)
         slot = t * 128 + lax.broadcasted_iota(jnp.int32, (8, 128), 1)
         live = jnp.where(slot < counts_ref[0], 1.0, 0.0).astype(jnp.float32)
 
         def store_value(row, rows_in, value):
             value_ref[row : row + rows_in, :] = (value * live)[:rows_in]
 
-        contract(b_ref, 0, 1, coef_ref, 2, store_value)
+        contract(b_ref, 0, 1, coef, 2, store_value)
         code, top = encode(value_ref[...])
         code_ref[t] = code
         top_ref[t] = jnp.broadcast_to(top, (8, 128))
@@ -325,9 +339,8 @@
                 copy.wait_recv()
             total = total + decode_square(got_code[d - 1, t], got_top[d - 1, t, 0:1, :])
         code, top = encode(jnp.sqrt(2.0 * total))
-        mine_code[t] = code
-        mine_top[t] = jnp.broadcast_to(top, (8, 128))
-        out_ref[rows(me), 128 * t : 128 * (t + 1)] = decode_square(code, top)
+        sum_code[me, t] = code
+        sum_top[me, t] = jnp.broadcast_to(top, (8, 128))
         for d in range(1, count):
             for copy in totals(d, t):
                 copy.start()
@@ -335,16 +348,22 @@
         for d in range(1, count):
             for copy in totals(d, t):
                 copy.wait_recv()
-            owner = lax.rem(me + count - d, count)
-            out_ref[rows(owner), 128 * t : 128 * (t + 1)] = decode_square(
-                sum_code[d - 1, t], sum_top[d - 1, t, 0:1, :]
-            )
-    for copy in (coarse_halo, waves_halo, fine_halo):
+    for copy in (*coarse_halo, waves_halo, fine_halo):
         copy.wait_send()
     for t in range(tiles):
         for d in range(1, count):
             for copy in partials(d, t) + totals(d, t):
                 copy.wait_send()
+
+
+def decode_kernel(code_ref, top_ref, out_ref):
+    count, tiles, chunk = code_ref.shape[:3]
+    for owner in range(count):
+        rows = min(chunk, ROWS - owner * chunk)
+        if rows > 0:
+            for t in range(tiles):
+                value = decode_square(code_ref[owner, t], top_ref[owner, t, 0:1, :])
+                out_ref[owner * chunk : owner * chunk + rows, 128 * t : 128 * (t + 1)] = value[:rows]
 
 
 def shards(coarse, wavelets, leaf_flags, child_key1, child_key2, counts):
@@ -358,36 +377,38 @@
     tiles = slots // 128
     peers = (count - 1, tiles)
     vmem = pl.BlockSpec(memory_space=pltpu.VMEM)
-    anywhere = pl.BlockSpec(memory_space=pl.ANY)
-    density = pl.pallas_call(
+    anywhere = pl.BlockSpec(memory_space=pltpu.HBM)
+    codes, tops = pl.pallas_call(
         lambda *refs: density_kernel(*refs, count=count, ranges=ranges, table=matrix, valued=valued),
-        out_shape=jax.ShapeDtypeStruct((padded, slots), jnp.float32),
+        out_shape=(
+            jax.ShapeDtypeStruct((count, tiles, chunk, 128), jnp.int16),
+            jax.ShapeDtypeStruct((count, tiles, 8, 128), jnp.float32),
+        ),
         in_specs=[pl.BlockSpec(memory_space=pltpu.SMEM), anywhere, anywhere, vmem, vmem, vmem],
-        out_specs=vmem,
+        out_specs=(vmem, vmem),
         scratch_shapes=[
-            pltpu.VMEM(coarse.shape, jnp.bfloat16),
+            pltpu.VMEM((8 * SEGMENT, 8, boxes), jnp.bfloat16),
             pltpu.VMEM(wavelets.shape, jnp.bfloat16),
-            pltpu.VMEM((2, 2, ROWS, 128), jnp.bfloat16),
-            pltpu.VMEM((2, 2, ROWS, 128), jnp.bfloat16),
+            pltpu.VMEM((2, 8 * SEGMENT, 128), jnp.bfloat16),
+            pltpu.VMEM((2, 8 * SEGMENT, 128), jnp.bfloat16),
+            pltpu.VMEM((2, ROWS, 128), jnp.bfloat16),
+            pltpu.VMEM((2, ROWS, 128), jnp.bfloat16),
+            pltpu.VMEM((8 * PADDED, 128), jnp.float32),
             pltpu.VMEM((4 * QUARTER, 128), jnp.float32),
             pltpu.VMEM((2, QUARTER, 128), jnp.bfloat16),
             pltpu.VMEM((2, QUARTER, 128), jnp.bfloat16),
             pltpu.VMEM((8, PADDED, 128), jnp.float32),
             pltpu.VMEM((4, PADDED, 128), jnp.float32),
             pltpu.VMEM((2, PADDED, 128), jnp.float32),
-            pltpu.VMEM((3 * 162, 8, 128), jnp.float32),
+            pltpu.VMEM((tiles + 1, 3 * 162, 8, 128), jnp.float32),
             pltpu.VMEM((padded, 128), jnp.float32),
             pltpu.VMEM((tiles, padded, 128), jnp.int16),
             pltpu.VMEM((tiles, 8, 128), jnp.float32),
             pltpu.VMEM(peers + (chunk, 128), jnp.int16),
             pltpu.VMEM(peers + (8, 128), jnp.float32),
-            pltpu.VMEM((tiles, chunk, 128), jnp.int16),
-            pltpu.VMEM((tiles, 8, 128), jnp.float32),
-            pltpu.VMEM(peers + (chunk, 128), jnp.int16),
-            pltpu.VMEM(peers + (8, 128), jnp.float32),
             pltpu.SemaphoreType.DMA((2,)),
-            pltpu.SemaphoreType.DMA((3,)),
-            pltpu.SemaphoreType.DMA((3,)),
+            pltpu.SemaphoreType.DMA((4,)),
+            pltpu.SemaphoreType.DMA((4,)),
         ]
         + [pltpu.SemaphoreType.DMA(peers)] * 8,
         compiler_params=pltpu.CompilerParams(
@@ -395,13 +416,18 @@
         ),
     )(
         counts,
-        coarse,
+        jnp.transpose(coarse[0], (1, 0, 2)),
         wavelets,
         leaf_flags,
         child_key1.reshape(1, boxes),
         child_key2.reshape(tiles, 1, 128),
     )
-    return density[:ROWS]
+    return pl.pallas_call(
+        decode_kernel,
+        out_shape=jax.ShapeDtypeStruct((ROWS, slots), jnp.float32),
+        in_specs=[vmem] * 2,
+        out_specs=vmem,
+    )(codes, tops)
 
 
 def solution(mesh):

time: 48.5 us -> 44.8 us (0.924)
  local copies, waits for them, and re-layouts: 4.77 us -> 0 us
  Pallas kernels: 42.8 us -> 44 us
    unnamed x1 -> x0, local copies, waits for them, and re-layouts: 2.73 us -> none
    slice x1 -> x0, local copies, waits for them, and re-layouts: 2.04 us -> none  [shards(): return density[:ROWS]]
    pallas_call x0 -> x1, Pallas kernels: none -> 1.97 us  [shards(): pl.pallas_call(decode_kernel, out_shape=jax.ShapeDtypeStruct((ROWS, slots...]
    pallas_call x1, Pallas kernels: 42.8 us -> 42 us  [shards(): pl.pallas_call(lambda *refs: density_kernel(*refs, count=count, ranges=ra...]
where the time goes in v1:
time: 44.8 us; the launch traced here: 44.6 us
  Pallas kernels  44 us (98%)
  between operations  0.66 us (1%)
    pallas_call x1, Pallas kernels, shards(): pl.pallas_call(lambda *refs: density_kernel(*refs, count=count, ranges=ra...  42 us
    pallas_call x1, Pallas kernels, shards(): pl.pallas_call(decode_kernel, out_shape=jax.ShapeDtypeStruct((ROWS, slots...  1.97 us

profile of v1, /device:TPU:0, one launch (start us, length us, event | category | flops | bytes accessed | tf_op | source)
XLA Modules:
  0.0 44.6 jit_solution(11488652307369240811)
XLA Ops:
  0.7 42.0 %shard_map.64 = (s16[4,2,192,128]{3,2,1,0:T(8,128)(2,1)}, f32[4,2,8,128]{3,2,1,0:T(8,128)}) custom-call(s32[1]{0:T(128)S(6)} %copy.7.refs_0_, bf16[729,8,128]{2,1,0:T(8,128)(2,1)} %bitcast.5, bf16[1,7,729,128]{3,2,1,0:T(8,128)(2,1)} %refs_2_.1, s32[1,128]{1,0:T(1,128)} %refs_3_.1, s32[1,128]{1,0:T(1,128)} %bitcast.7, s32[2,1,128]{2,1,0:T(1,128)} %bitcast.6), custom_call_target="tpu_custom_call" | custom-call | tf_op jit(solution)/shard_map/pallas_call | solution.py:381
  42.6 2.0 %shard_map.65 = f32[729,256]{1,0:T(8,128)} custom-call(s16[4,2,192,128]{3,2,1,0:T(8,128)(2,1)} %get-tuple-element.7.code_ref, f32[4,2,8,128]{3,2,1,0:T(8,128)} %get-tuple-element.8.top_ref), custom_call_target="tpu_custom_call" | custom-call | tf_op jit(solution)/shard_map/pallas_call | solution.py:425
